TPU v7x, 512 devices: a whole 4x4x16 slice. The times are simulated.
512 devices in a mesh: node: 16 (over x, y), rows: 32 (over z, core).
Axes of the slice: x: 4, y: 4, z: 16, core: 2. Of those that a mesh axis runs over, the one named last changes fastest.
Arguments:
- subspace: bfloat16 [24576, 256], P('rows'), may hold values from -6 to 6
- inverse: bfloat16 [16, 2, 24576, 768], P('node', None, 'rows')
- weights: float32 [16, 2], P('node'), may hold values from 0.25 to 1
- diag_tiles: float32 [24576, 128], P('rows'), may hold values from -0.5 to 0.5
- upper_tiles: float32 [24576, 128], P('rows'), may hold values from -0.5 to 0.5
Outputs:
- subspace_out: float32 [24576, 256], P('rows')
- projected: float32 [2, 256, 256], replicated
All inputs are finite; a program needn't handle non-finite values.
Results may differ from a plain program's by a relative error of at most 0.0025.
Values may be sent and summed in bfloat16 or wider, within the bound.
A program may use at most 64 MiB of HBM per device.

v0:
```python
import functools

import jax
import jax.numpy as jnp
from jax import lax
from jax.experimental import pallas as pl
from jax.experimental.pallas import tpu as pltpu
from jax.sharding import PartitionSpec as P

ITERS = 2
MESH = pl.DeviceIdType.MESH
F32, BF16 = jnp.float32, jnp.bfloat16
precise = lax.Precision.HIGHEST


def dot(a, b, ca=1, cb=0, precision=None):
    return lax.dot_general(
        a, b, (((ca,), (cb,)), ((), ())), precision=precision, preferred_element_type=F32
    )


def split3(x):
    high = x.astype(BF16)
    rest = x - high.astype(F32)
    middle = rest.astype(BF16)
    low = (rest - middle.astype(F32)).astype(BF16)
    return high, middle, low


def panel_step(a, k, size):
    r0 = 8 * k
    half, lane0 = r0 // 128, r0 % 128
    halves = size // 128
    row = [[jnp.broadcast_to(a[h, r0 + i : r0 + i + 1, :], (8, 128)) for h in range(halves)] for i in range(8)]
    e = [
        [jnp.broadcast_to(row[i][half][:, lane0 + j : lane0 + j + 1], (8, 128)) for j in range(i + 1)]
        for i in range(8)
    ]
    t = [[None] * 8 for _ in range(8)]
    for j in range(8):
        r = lax.rsqrt(e[j][j])
        for q in range(j):
            t[j][q] = t[j][q] * r
        t[j][j] = r
        m = {i: e[i][j] * r for i in range(j + 1, 8)}
        for i in range(j + 1, 8):
            for q in range(j + 1, i + 1):
                e[i][q] = e[i][q] - m[i] * m[q]
            for q in range(j + 1):
                prev = t[i][q]
                t[i][q] = -m[i] * t[j][q] if prev is None else prev - m[i] * t[j][q]
    sub = lax.broadcasted_iota(jnp.int32, (8, 128), 0)
    lane = lax.broadcasted_iota(jnp.int32, (8, 128), 1)
    out = [jnp.zeros((8, 128), F32) for _ in range(halves)]
    diag = jnp.zeros((8, 128), F32)
    for q in range(8):
        col = jnp.zeros((8, 128), F32)
        for i in range(q, 8):
            col = jnp.where(sub == i, t[i][q], col)
        for h in range(halves):
            out[h] = out[h] + col * row[q][h]
        diag = jnp.where(lane == lane0 + q, col, diag)
    inside = (lane >= lane0) & (lane < lane0 + 8)
    new = [jnp.where(inside, diag, out[h]) if h == half else out[h] for h in range(halves)]
    for h in range(halves):
        a[h, r0 : r0 + 8, :] = new[h]
    if r0 + 8 >= size:
        return
    below = size - r0 - 8
    base = 128 * ((r0 + 8) // 128)
    lh, lm, ll = split3(jnp.concatenate([out[h] for h in range(base // 128, halves)], axis=1))
    rh, rm, rl = split3(jnp.concatenate(new, axis=1))
    left = jnp.concatenate([lh, lh, lm, lh, ll, lm], axis=0)
    right = jnp.concatenate([rh, rm, rh, rl, rh, rm], axis=0)
    update = dot(left, right, 0, 0)
    off = r0 + 8 - base
    for h in range(halves):
        old = a[h, r0 + 8 : size, :]
        if h == half:
            lanes = lax.broadcasted_iota(jnp.int32, (below, 128), 1)
            old = jnp.where((lanes >= lane0) & (lanes < lane0 + 8), 0.0, old)
        a[h, r0 + 8 : size, :] = old - update[off:, 128 * h : 128 * h + 128]


def packed(whole):
    half = whole.shape[0] // 2
    rows = lax.broadcasted_iota(jnp.int32, (half, half), 0)
    columns = lax.broadcasted_iota(jnp.int32, (half, half), 1)
    last = whole[half:, half:]
    row = jnp.sum(jnp.where(rows == columns, last, 0.0), axis=0, keepdims=True)
    return jnp.where(rows <= columns, whole[:half, :half], last), whole[:half, half:], row


def unpacked(first, second, row):
    half = first.shape[0]
    rows = lax.broadcasted_iota(jnp.int32, (half, half), 0)
    columns = lax.broadcasted_iota(jnp.int32, (half, half), 1)
    turned = first.T
    last = jnp.where(rows > columns, first, jnp.where(rows < columns, turned, row))
    return jnp.where(rows <= columns, first, turned), second, last


def kernel(
    nodes, parts, scale,
    subspace, inverse, weights, diag_in, upper_in, out, projected,
    current, blocks, diag, upper, firsts, ups, from_next, from_prior, edge,
    term, ra, rb, pa, pb, qa, qb, field, next_rows, imaged,
    block, mine, pair, pk, grs, zb, res, rest, a, inv, ortho, proj,
    load, tip_send, tip_recv, rsa_send, rsa_recv, rsb_send, rsb_recv,
    rsc_send, rsc_recv, rsd_send, rsd_recv,
    aga_send, aga_recv, agb_send, agb_recv, agc_send, agc_recv, agd_send, agd_recv,
    row_send, row_recv, pair_send, pair_recv, grs_send, grs_recv,
    z_send, z_recv, all_send, all_recv, fin_send, fin_recv,
):
    j, p = lax.axis_index("node"), lax.axis_index("rows")
    side = int(round(nodes**0.5))
    x, y = j // side, lax.rem(j, side)
    core = lax.rem(p, 2)
    sibling = p + 1 - 2 * core
    up, down = lax.rem(p + 1, parts), lax.rem(p + parts - 1, parts)
    cross = lax.rem(p + parts - 1 + 2 * core, parts)
    chips = parts // 2
    z = p // 2
    size, columns = current.shape
    band = diag.shape[1]
    piece = size // nodes // 2
    half = columns // 2
    share = half // nodes

    def each(start, stop, act):
        def step(k, carry):
            act(k)
            return carry

        lax.fori_loop(start, stop, step, 0)

    def turn(value, k, count):
        return lax.rem(value + k, count)

    def copy(src, dst, send, recv, device):
        return pltpu.make_async_remote_copy(
            src_ref=src, dst_ref=dst, send_sem=send, recv_sem=recv, device_id=device, device_id_type=MESH
        )

    loads = [
        pltpu.make_async_copy(subspace, current, load.at[0]),
        pltpu.make_async_copy(inverse, blocks, load.at[1]),
        pltpu.make_async_copy(upper_in, upper, load.at[2]),
        pltpu.make_async_copy(diag_in, diag, load.at[3]),
    ]
    for item in loads:
        item.start()
    barrier = pltpu.get_barrier_semaphore()

    def greet(device):
        pl.semaphore_signal(barrier, inc=1, device_id=device, device_id_type=MESH)

    each(1, chips, lambda k: greet((j, turn(p, 2 * k, parts))))
    each(1, nodes, lambda k: greet((turn(j, k, nodes), p)))
    greet((j, cross))
    greet((j, sibling))
    for item in loads:
        item.wait()
    w0, w1 = weights[0, 0], weights[0, 1]

    def tips():
        coupling = upper[size - band :, :]
        for part in range(2):
            last = dot(blocks[part, size - band :, :], current[...]).astype(BF16).astype(F32)
            ups[part] = dot(coupling, last, 0, 0, precise).astype(BF16)
            firsts[part] = dot(blocks[part, :band, :], current[...]).astype(BF16)

    tips()
    pl.semaphore_wait(barrier, nodes - 1 + chips - 1 + 2)

    def pair_copy(it, m):
        return copy(block.at[m], pair.at[it, m], pair_send.at[it, m], pair_recv.at[it, m], (j, sibling))

    def pack_start(it, m, whole):
        first, second, row = packed(whole)
        mine[m] = jnp.where(core == 0, first, second)
        block[m, :half, :] = jnp.where(core == 0, second, first)
        block[m, half:, :] = jnp.broadcast_to(row, (8, half))
        pair_copy(it, m).start()

    def pack_sum(it, m):
        pair_copy(it, m).wait()
        total = mine[m] + pair[it, m, :half, :]
        pk[m, :, :share, :] = total.reshape(nodes, share, half)
        row = block[m, half:, :] + pair[it, m, half:, :]
        pk[m, :, share:, :] = jnp.broadcast_to(row[None], (nodes, 8, half))

    slice_rows = pl.ds(0, share + 1)

    def grs_copy(it, source, to):
        return copy(
            pk.at[0, to, slice_rows, :], grs.at[it, source, slice_rows, :],
            grs_send.at[it, to], grs_recv.at[it, source], (to, p),
        )

    def z_copy(it, m, source, to):
        here = zb.at[it, m, source, slice_rows, :]
        return copy(here, here, z_send.at[it, m, to], z_recv.at[it, m, source], (j, 2 * to + core))

    def z_start(it, m, value):
        zb[it, m, z, slice_rows, :] = value
        each(1, chips, lambda k: z_copy(it, m, z, turn(z, k, chips)).start())

    def all_copy(it, m, source, to):
        here = res.at[it, m, core, pl.ds(pl.multiple_of(source * share, 8), share), :]
        return copy(here, here, all_send.at[it, m, to], all_recv.at[it, m, source], (to, p))

    def z_finish(it, m):
        def add(k, total):
            source = turn(z, chips - k, chips)
            z_copy(it, m, source, source).wait_recv()
            return total + zb[it, m, source, slice_rows, :]

        total = lax.fori_loop(1, chips, add, zb[it, m, z, slice_rows, :])
        rest[it, m] = jnp.broadcast_to(total[share : share + 1, :], (8, half))
        res[it, m, core, pl.ds(pl.multiple_of(j * share, 8), share), :] = total[:share, :]
        each(1, nodes, lambda k: all_copy(it, m, j, turn(j, k, nodes)).start())

    def fin_copy(it, m, which):
        here = res.at[it, m, which]
        return copy(here, here, fin_send.at[it, m], fin_recv.at[it, m], (j, sibling))

    def all_finish(it, m):
        def wait(k):
            source = turn(j, nodes - k, nodes)
            all_copy(it, m, source, source).wait_recv()

        each(1, nodes, wait)
        fin_copy(it, m, core).start()

    def summed(it, m):
        fin_copy(it, m, 1 - core).wait_recv()
        return unpacked(res[it, m, 0], res[it, m, 1], rest[it, m, 0:1, :])

    def project(it):
        first, second, last = summed(it, 1)
        whole = jnp.concatenate(
            [jnp.concatenate([first, second], axis=1), jnp.concatenate([second.T, last], axis=1)], axis=0
        )
        left = dot(inv[it], whole * scale, 1, 0, precise)
        proj[it] = dot(left, inv[it], 1, 1, precise)

    def drained(it):
        tip_down, tip_up = tip_copies(it)
        tip_down.wait_send()
        tip_up.wait_send()
        row_copy(it).wait_send()

        def over_side(k):
            xx, yy = turn(x, k, side), turn(y, k, side)
            rsa_copy(it, xx, x).wait_send()
            rsc_copy(it, yy, y).wait_send()
            rsd_copy(it, xx, x).wait_send()
            aga_copy(it, xx, x).wait_send()
            agb_copy(it, yy, y).wait_send()
            agc_copy(it, yy, y).wait_send()
            agd_copy(it, xx, x).wait_send()
            each(0, side, lambda g: rsb_copy(it, g, yy, y).wait_send())

        each(1, side, over_side)

        def over_nodes(k):
            to = turn(j, k, nodes)
            grs_copy(it, j, to).wait_send()
            all_copy(it, 0, j, to).wait_send()

        each(1, nodes, over_nodes)
        each(1, chips, lambda k: z_copy(it, 0, z, turn(z, k, chips)).wait_send())
        each(1, chips, lambda k: z_copy(it, 1, z, turn(z, k, chips)).wait_send())
        fin_copy(it, 0, core).wait_send()

    def projected_drained(it):
        each(1, nodes, lambda k: all_copy(it, 1, j, turn(j, k, nodes)).wait_send())
        fin_copy(it, 1, core).wait_send()

    def tip_copies(it):
        return (
            copy(firsts, from_next.at[it], tip_send.at[it, 0], tip_recv.at[it, 0], (j, down)),
            copy(ups, from_prior.at[it], tip_send.at[it, 1], tip_recv.at[it, 1], (j, up)),
        )

    def rsa_copy(it, g, source):
        return copy(term.at[g, :, 0], ra.at[it, source], rsa_send.at[it, g], rsa_recv.at[it, source], (g * side + y, p))

    def rsb_copy(it, g, to, source):
        return copy(
            term.at[g, to, 1], rb.at[it, source, g], rsb_send.at[it, to, g], rsb_recv.at[it, source, g], (x * side + to, p)
        )

    def rsc_copy(it, to, source):
        return copy(pa.at[to], qa.at[it, source], rsc_send.at[it, to], rsc_recv.at[it, source], (x * side + to, p))

    def rsd_copy(it, to, source):
        return copy(pb.at[to], qb.at[it, source], rsd_send.at[it, to], rsd_recv.at[it, source], (to * side + y, p))

    def aga_copy(it, to, source):
        here = field.at[it, source, y, 0]
        return copy(here, here, aga_send.at[it, to], aga_recv.at[it, source], (to * side + y, p))

    def agb_copy(it, to, source):
        here = field.at[it, x, source, 1]
        return copy(here, here, agb_send.at[it, to], agb_recv.at[it, source], (x * side + to, p))

    def agc_copy(it, to, source):
        here = field.at[it, :, source, 0]
        return copy(here, here, agc_send.at[it, to], agc_recv.at[it, source], (x * side + to, p))

    def agd_copy(it, to, source):
        here = field.at[it, source, :, 1]
        return copy(here, here, agd_send.at[it, to], agd_recv.at[it, source], (to * side + y, p))

    def row_copy(it):
        return copy(edge, next_rows.at[it], row_send.at[it], row_recv.at[it], (j, down))

    tile = size // side

    def iteration(it, carry):
        tip_down, tip_up = tip_copies(it)
        tip_up.start()
        tip_down.start()
        for g in range(side):
            rows = pl.ds(g * tile, tile)
            value = w0 * dot(blocks[0, rows, :], current[...]) - w1 * dot(blocks[1, rows, :], current[...])
            term[g] = value.reshape(side, 2, piece, columns)

        @pl.when(it > 0)
        def _():
            all_finish(it - 1, 1)
            project(it - 1)
            projected_drained(it - 1)

        tip_down.wait_recv()
        coupling = upper[size - band :, :]
        bottom = []
        for part in range(2):
            below = dot(coupling, from_next[it, part].astype(F32), 1, 0, precise)
            bottom.append(jnp.where(p == parts - 1, 0.0, below).astype(BF16))
        tip_up.wait_recv()
        top = [jnp.where(p == 0, 0.0, from_prior[it, part].astype(F32)).astype(BF16) for part in range(2)]
        top, bottom = jnp.concatenate(top, axis=1), jnp.concatenate(bottom, axis=1)

        def group(t):
            g = turn(x, t + 1, side)
            rows = pl.ds(pl.multiple_of(g * tile, 8), tile)
            real = dot(blocks[0, rows, :band], top) + dot(blocks[0, rows, size - band :], bottom)
            imag = dot(blocks[1, rows, :band], top) + dot(blocks[1, rows, size - band :], bottom)
            change = w0 * (real[:, :columns] - imag[:, columns:]) - w1 * (real[:, columns:] + imag[:, :columns])
            term[g] = term[g] + change.reshape(side, 2, piece, columns)

            @pl.when(g != x)
            def _():
                rsa_copy(it, g, x).start()

            each(1, side, lambda k: rsb_copy(it, g, turn(y, k, side), y).start())

        each(0, side, group)

        def add_a(k, total):
            source = turn(x, side - k, side)
            rsa_copy(it, source, source).wait_recv()
            return total + ra[it, source]

        pa[...] = lax.fori_loop(1, side, add_a, term[x, :, 0])
        each(1, side, lambda k: rsc_copy(it, turn(y, k, side), y).start())

        def add_b(k, total):
            source = turn(y, side - k, side)
            each(0, side, lambda g: rsb_copy(it, g, source, source).wait_recv())
            return total + rb[it, source]

        pb[...] = lax.fori_loop(1, side, add_b, term[:, y, 1])
        each(1, side, lambda k: rsd_copy(it, turn(x, k, side), x).start())

        def add_c(k, total):
            source = turn(y, side - k, side)
            rsc_copy(it, source, source).wait_recv()
            return total + qa[it, source]

        field[it, x, y, 0] = lax.fori_loop(1, side, add_c, pa[y])

        def add_d(k, total):
            source = turn(x, side - k, side)
            rsd_copy(it, source, source).wait_recv()
            return total + qb[it, source]

        field[it, x, y, 1] = lax.fori_loop(1, side, add_d, pb[x])

        own = field[it, x, y].reshape(2 * piece, columns)
        pack_start(it, 0, dot(own, own, 0, 0, precise))
        pack_sum(it, 0)
        each(1, nodes, lambda k: grs_copy(it, j, turn(j, k, nodes)).start())

        def add_g(k, total):
            source = turn(j, nodes - k, nodes)
            grs_copy(it, source, source).wait_recv()
            return total + grs[it, source, slice_rows, :]

        z_start(it, 0, lax.fori_loop(1, nodes, add_g, pk[0, j, slice_rows, :]))

        def ag_first(k):
            aga_copy(it, turn(x, k, side), x).start()
            agb_copy(it, turn(y, k, side), y).start()

        each(1, side, ag_first)

        def ag_first_wait(k):
            aga_copy(it, turn(x, k, side), turn(x, k, side)).wait_recv()

        each(1, side, ag_first_wait)
        each(1, side, lambda k: agc_copy(it, turn(y, k, side), y).start())

        def ag_second_wait(k):
            agb_copy(it, turn(y, k, side), turn(y, k, side)).wait_recv()

        each(1, side, ag_second_wait)
        each(1, side, lambda k: agd_copy(it, turn(x, k, side), x).start())
        z_finish(it, 0)

        def ag_last_wait(k):
            agc_copy(it, turn(y, k, side), turn(y, k, side)).wait_recv()
            agd_copy(it, turn(x, k, side), turn(x, k, side)).wait_recv()

        each(1, side, ag_last_wait)
        whole = field[it].reshape(size, columns)
        edge[...] = whole[:band, :]
        row_copy(it).start()
        tiles = size // band
        for t in range(tiles - 1):
            rows = slice(t * band, t * band + band)
            imaged[rows, :] = dot(0.5 * diag[rows, :], whole[rows, :], 1, 0, precise) + dot(
                upper[rows, :], whole[t * band + band : t * band + 2 * band, :], 1, 0, precise
            )
        rows = slice(size - band, size)
        near = dot(0.5 * diag[rows, :], whole[rows, :], 1, 0, precise)
        row_copy(it).wait_recv()
        after = jnp.where(p == parts - 1, 0.0, next_rows[it])
        imaged[rows, :] = near + dot(upper[rows, :], after, 1, 0, precise)
        product = dot(whole, imaged[...], 0, 0, precise)
        pack_start(it, 1, product + product.T)

        all_finish(it, 0)
        pack_sum(it, 1)
        z_start(it, 1, pk[1, j, slice_rows, :])
        first, second, last = summed(it, 0)
        a[0, :half, :] = first * scale
        a[1, :half, :] = second * scale
        a[0, half:, :] = jnp.zeros((half, half), F32)
        a[1, half:, :] = last * scale
        steps = columns // 8
        for k in range(steps):
            if k == (5 * steps) // 8:
                z_finish(it, 1)
            panel_step(a, k, columns)
        rows = lax.broadcasted_iota(jnp.int32, (columns, columns), 0)
        cols = lax.broadcasted_iota(jnp.int32, (columns, columns), 1)
        factor = jnp.where(rows >= cols, jnp.concatenate([a[0], a[1]], axis=1), 0.0)
        inv[it] = factor
        for g in range(side):
            rows = pl.ds(g * tile, tile)
            value = dot(field[it, g].reshape(tile, columns), factor, 1, 1, precise)
            ortho[rows, :] = value
            current[rows, :] = value.astype(BF16)
        drained(it)

        @pl.when(it < ITERS - 1)
        def _():
            tips()

        return carry

    lax.fori_loop(0, ITERS, iteration, 0)
    store = pltpu.make_async_copy(ortho, out, load.at[0])
    store.start()
    all_finish(ITERS - 1, 1)
    project(ITERS - 1)
    projected_drained(ITERS - 1)
    last_store = pltpu.make_async_copy(proj, projected, load.at[1])
    last_store.start()
    store.wait()
    last_store.wait()


def per_device(subspace, inverse, weights, diag_tiles, upper_tiles):
    nodes, parts = lax.axis_size("node"), lax.axis_size("rows")
    rows, columns = subspace.shape
    band = diag_tiles.shape[1]
    side = int(round(nodes**0.5))
    piece = rows // nodes // 2
    half = columns // 2
    share = half // nodes
    chips = parts // 2
    n = ITERS
    vmem, dma = pltpu.VMEM, pltpu.SemaphoreType.DMA
    anywhere = pl.BlockSpec(memory_space=pl.ANY)
    tip = (2, band, columns)
    scratch = [
        vmem((rows, columns), BF16), vmem((2, rows, rows), BF16), vmem((rows, band), F32), vmem((rows, band), F32),
        vmem(tip, BF16), vmem(tip, BF16), vmem((n, *tip), BF16), vmem((n, *tip), BF16), vmem((band, columns), F32),
        vmem((side, side, 2, piece, columns), F32),
        vmem((n, side, side, piece, columns), F32), vmem((n, side, side, piece, columns), F32),
        vmem((side, piece, columns), F32), vmem((side, piece, columns), F32),
        vmem((n, side, piece, columns), F32), vmem((n, side, piece, columns), F32),
        vmem((n, side, side, 2, piece, columns), F32), vmem((n, band, columns), F32), vmem((rows, columns), F32),
        vmem((2, half + 8, half), F32), vmem((2, half, half), F32), vmem((n, 2, half + 8, half), F32),
        vmem((2, nodes, share + 8, half), F32), vmem((n, nodes, share + 8, half), F32),
        vmem((n, 2, chips, share + 8, half), F32), vmem((n, 2, 2, half, half), F32), vmem((n, 2, 8, half), F32),
        vmem((2, columns, half), F32), vmem((n, columns, columns), F32), vmem((rows, columns), F32),
        vmem((n, columns, columns), F32),
        dma((4,)), dma((n, 2)), dma((n, 2)), dma((n, side)), dma((n, side)), dma((n, side, side)), dma((n, side, side)),
    ]
    scratch += [dma((n, side))] * 12
    scratch += [dma((n,)), dma((n,)), dma((n, 2)), dma((n, 2)), dma((n, nodes)), dma((n, nodes))]
    scratch += [dma((n, 2, chips))] * 2 + [dma((n, 2, nodes))] * 2 + [dma((n, 2))] * 2
    return pl.pallas_call(
        functools.partial(kernel, nodes, parts, 1.0 / (rows * parts)),
        out_shape=(
            jax.ShapeDtypeStruct((rows, columns), F32),
            jax.ShapeDtypeStruct((n, columns, columns), F32),
        ),
        in_specs=[anywhere, anywhere, pl.BlockSpec(memory_space=pltpu.SMEM), anywhere, anywhere],
        out_specs=(anywhere, anywhere),
        scratch_shapes=scratch,
        compiler_params=pltpu.CompilerParams(
            collective_id=0, has_side_effects=True, vmem_limit_bytes=60 * 1024 * 1024
        ),
    )(subspace, inverse[0], weights, diag_tiles, upper_tiles)


def solution(mesh):
    placed = (
        P("rows", None),
        P("node", None, "rows", None),
        P("node", None),
        P("rows", None),
        P("rows", None),
    )
    return jax.shard_map(
        per_device, mesh=mesh, in_specs=placed, out_specs=(P("rows", None), P()), check_vma=False
    )
```

profile of v0, /device:TPU:1, one launch (start us, length us, event | category | flops | bytes accessed | tf_op | source)
XLA Modules:
  0.0 138.9 jit_solution(18385265416362952480)
XLA Ops:
  0.6 134.3 %shard_map.68 = (f32[768,256]{1,0:T(8,128)}, f32[2,256,256]{2,1,0:T(8,128)}) custom-call(bf16[768,256]{1,0:T(8,128)(2,1)} %subspace.1, bf16[2,768,768]{2,1,0:T(8,128)(2,1)} %bitcast.1, f32[1,2]{1,0:T(1,128)} %weights.1, f32[768,128]{1,0:T(8,128)} %diag_in.1, f32[768,128]{1,0:T(8,128)} %upper_in.1), custom_call_target="tpu_custom_call" | custom-call | tf_op jit(solution)/shard_map/pallas_call | solution.py:519
  135.0 2.1 %copy.9 = f32[768,256]{1,0:T(8,128)} copy(f32[768,256]{1,0:T(8,128)} %get-tuple-element.4) | data formatting | bytes 1572864
  137.0 1.9 %copy.10 = f32[2,256,256]{2,1,0:T(8,128)} copy(f32[2,256,256]{2,1,0:T(8,128)} %get-tuple-element.5) | data formatting | bytes 1048576
where the time goes:
time: 139 us
  Pallas kernels  134 us (96%)
  local copies, waits for them, and re-layouts  3.93 us (3%)
    pallas_call x1, Pallas kernels, per_device(): pl.pallas_call(functools.partial(kernel, nodes, parts, 1.0 / (rows * part...  134 us
    unnamed x2, local copies, waits for them, and re-layouts  3.93 us

commit v1 on v0

--- a/solution.py
+++ b/solution.py
@@ -105,7 +105,7 @@
     subspace, inverse, weights, diag_in, upper_in, out, projected,
     current, blocks, diag, upper, firsts, ups, from_next, from_prior, edge,
     term, ra, rb, pa, pb, qa, qb, field, next_rows, imaged,
-    block, mine, pair, pk, grs, zb, res, rest, a, inv, ortho, proj,
+    block, mine, pair, pk, grs, zb, res, rest, a, inv,
     load, tip_send, tip_recv, rsa_send, rsa_recv, rsb_send, rsb_recv,
     rsc_send, rsc_recv, rsd_send, rsd_recv,
     aga_send, aga_recv, agb_send, agb_recv, agc_send, agc_recv, agd_send, agd_recv,
@@ -128,11 +128,13 @@
     share = half // nodes
 
     def each(start, stop, act):
-        def step(k, carry):
+        for k in range(start, stop):
             act(k)
-            return carry
-
-        lax.fori_loop(start, stop, step, 0)
+
+    def added(start, stop, add, total):
+        for k in range(start, stop):
+            total = add(k, total)
+        return total
 
     def turn(value, k, count):
         return lax.rem(value + k, count)
@@ -163,15 +165,20 @@
         item.wait()
     w0, w1 = weights[0, 0], weights[0, 1]
 
-    def tips():
+    def tips(it, ready):
+        tip_down, tip_up = tip_copies(it)
         coupling = upper[size - band :, :]
+        for part in range(2):
+            firsts[part] = dot(blocks[part, :band, :], current[...]).astype(BF16)
+        if ready:
+            tip_down.start()
         for part in range(2):
             last = dot(blocks[part, size - band :, :], current[...]).astype(BF16).astype(F32)
             ups[part] = dot(coupling, last, 0, 0, precise).astype(BF16)
-            firsts[part] = dot(blocks[part, :band, :], current[...]).astype(BF16)
-
-    tips()
-    pl.semaphore_wait(barrier, nodes - 1 + chips - 1 + 2)
+        if not ready:
+            pl.semaphore_wait(barrier, nodes - 1 + chips - 1 + 2)
+            tip_down.start()
+        tip_up.start()
 
     def pair_copy(it, m):
         return copy(block.at[m], pair.at[it, m], pair_send.at[it, m], pair_recv.at[it, m], (j, sibling))
@@ -216,7 +223,7 @@
             z_copy(it, m, source, source).wait_recv()
             return total + zb[it, m, source, slice_rows, :]
 
-        total = lax.fori_loop(1, chips, add, zb[it, m, z, slice_rows, :])
+        total = added(1, chips, add, zb[it, m, z, slice_rows, :])
         rest[it, m] = jnp.broadcast_to(total[share : share + 1, :], (8, half))
         res[it, m, core, pl.ds(pl.multiple_of(j * share, 8), share), :] = total[:share, :]
         each(1, nodes, lambda k: all_copy(it, m, j, turn(j, k, nodes)).start())
@@ -243,12 +250,9 @@
             [jnp.concatenate([first, second], axis=1), jnp.concatenate([second.T, last], axis=1)], axis=0
         )
         left = dot(inv[it], whole * scale, 1, 0, precise)
-        proj[it] = dot(left, inv[it], 1, 1, precise)
+        projected[it] = dot(left, inv[it], 1, 1, precise)
 
     def drained(it):
-        tip_down, tip_up = tip_copies(it)
-        tip_down.wait_send()
-        tip_up.wait_send()
         row_copy(it).wait_send()
 
         def over_side(k):
@@ -320,9 +324,10 @@
     tile = size // side
 
     def iteration(it, carry):
-        tip_down, tip_up = tip_copies(it)
-        tip_up.start()
-        tip_down.start()
+        @pl.when(it > 0)
+        def _():
+            drained(it - 1)
+
         for g in range(side):
             rows = pl.ds(g * tile, tile)
             value = w0 * dot(blocks[0, rows, :], current[...]) - w1 * dot(blocks[1, rows, :], current[...])
@@ -334,22 +339,28 @@
             project(it - 1)
             projected_drained(it - 1)
 
-        tip_down.wait_recv()
+        tip_down, tip_up = tip_copies(it)
+        tip_down.wait()
         coupling = upper[size - band :, :]
         bottom = []
         for part in range(2):
-            below = dot(coupling, from_next[it, part].astype(F32), 1, 0, precise)
-            bottom.append(jnp.where(p == parts - 1, 0.0, below).astype(BF16))
-        tip_up.wait_recv()
-        top = [jnp.where(p == 0, 0.0, from_prior[it, part].astype(F32)).astype(BF16) for part in range(2)]
-        top, bottom = jnp.concatenate(top, axis=1), jnp.concatenate(bottom, axis=1)
+            below = dot(coupling, from_next[it, part].astype(F32), 1, 0, precise).astype(BF16)
+            bottom.append(jnp.where(p == parts - 1, 0.0, below.astype(F32)))
+        tip_up.wait()
+        top = [jnp.where(p == 0, 0.0, from_prior[it, part].astype(F32)) for part in range(2)]
+        edges = jnp.concatenate(
+            [w0 * e[0] - w1 * e[1] for e in (top, bottom)] + [-w0 * e[1] - w1 * e[0] for e in (top, bottom)], axis=0
+        )
+        edge_high = edges.astype(BF16)
+        edge_low = (edges - edge_high.astype(F32)).astype(BF16)
 
         def group(t):
             g = turn(x, t + 1, side)
             rows = pl.ds(pl.multiple_of(g * tile, 8), tile)
-            real = dot(blocks[0, rows, :band], top) + dot(blocks[0, rows, size - band :], bottom)
-            imag = dot(blocks[1, rows, :band], top) + dot(blocks[1, rows, size - band :], bottom)
-            change = w0 * (real[:, :columns] - imag[:, columns:]) - w1 * (real[:, columns:] + imag[:, :columns])
+            corner = jnp.concatenate(
+                [blocks[part, rows, at] for part in range(2) for at in (slice(0, band), slice(size - band, size))], axis=1
+            )
+            change = dot(corner, edge_high) + dot(corner, edge_low)
             term[g] = term[g] + change.reshape(side, 2, piece, columns)
 
             @pl.when(g != x)
@@ -365,7 +376,7 @@
             rsa_copy(it, source, source).wait_recv()
             return total + ra[it, source]
 
-        pa[...] = lax.fori_loop(1, side, add_a, term[x, :, 0])
+        pa[...] = added(1, side, add_a, term[x, :, 0])
         each(1, side, lambda k: rsc_copy(it, turn(y, k, side), y).start())
 
         def add_b(k, total):
@@ -373,7 +384,7 @@
             each(0, side, lambda g: rsb_copy(it, g, source, source).wait_recv())
             return total + rb[it, source]
 
-        pb[...] = lax.fori_loop(1, side, add_b, term[:, y, 1])
+        pb[...] = added(1, side, add_b, term[:, y, 1])
         each(1, side, lambda k: rsd_copy(it, turn(x, k, side), x).start())
 
         def add_c(k, total):
@@ -381,14 +392,14 @@
             rsc_copy(it, source, source).wait_recv()
             return total + qa[it, source]
 
-        field[it, x, y, 0] = lax.fori_loop(1, side, add_c, pa[y])
+        field[it, x, y, 0] = added(1, side, add_c, pa[y])
 
         def add_d(k, total):
             source = turn(x, side - k, side)
             rsd_copy(it, source, source).wait_recv()
             return total + qb[it, source]
 
-        field[it, x, y, 1] = lax.fori_loop(1, side, add_d, pb[x])
+        field[it, x, y, 1] = added(1, side, add_d, pb[x])
 
         own = field[it, x, y].reshape(2 * piece, columns)
         pack_start(it, 0, dot(own, own, 0, 0, precise))
@@ -400,7 +411,7 @@
             grs_copy(it, source, source).wait_recv()
             return total + grs[it, source, slice_rows, :]
 
-        z_start(it, 0, lax.fori_loop(1, nodes, add_g, pk[0, j, slice_rows, :]))
+        z_start(it, 0, added(1, nodes, add_g, pk[0, j, slice_rows, :]))
 
         def ag_first(k):
             aga_copy(it, turn(x, k, side), x).start()
@@ -453,7 +464,7 @@
         a[1, half:, :] = last * scale
         steps = columns // 8
         for k in range(steps):
-            if k == (5 * steps) // 8:
+            if k == (3 * steps) // 4 - 1:
                 z_finish(it, 1)
             panel_step(a, k, columns)
         rows = lax.broadcasted_iota(jnp.int32, (columns, columns), 0)
@@ -463,26 +474,21 @@
         for g in range(side):
             rows = pl.ds(g * tile, tile)
             value = dot(field[it, g].reshape(tile, columns), factor, 1, 1, precise)
-            ortho[rows, :] = value
+            out[rows, :] = value
             current[rows, :] = value.astype(BF16)
-        drained(it)
 
         @pl.when(it < ITERS - 1)
         def _():
-            tips()
+            tips(it + 1, True)
 
         return carry
 
+    tips(0, False)
     lax.fori_loop(0, ITERS, iteration, 0)
-    store = pltpu.make_async_copy(ortho, out, load.at[0])
-    store.start()
     all_finish(ITERS - 1, 1)
     project(ITERS - 1)
     projected_drained(ITERS - 1)
-    last_store = pltpu.make_async_copy(proj, projected, load.at[1])
-    last_store.start()
-    store.wait()
-    last_store.wait()
+    drained(ITERS - 1)
 
 
 def per_device(subspace, inverse, weights, diag_tiles, upper_tiles):
@@ -509,8 +515,7 @@
         vmem((2, half + 8, half), F32), vmem((2, half, half), F32), vmem((n, 2, half + 8, half), F32),
         vmem((2, nodes, share + 8, half), F32), vmem((n, nodes, share + 8, half), F32),
         vmem((n, 2, chips, share + 8, half), F32), vmem((n, 2, 2, half, half), F32), vmem((n, 2, 8, half), F32),
-        vmem((2, columns, half), F32), vmem((n, columns, columns), F32), vmem((rows, columns), F32),
-        vmem((n, columns, columns), F32),
+        vmem((2, columns, half), F32), vmem((n, columns, columns), F32),
         dma((4,)), dma((n, 2)), dma((n, 2)), dma((n, side)), dma((n, side)), dma((n, side, side)), dma((n, side, side)),
     ]
     scratch += [dma((n, side))] * 12
@@ -523,10 +528,10 @@
             jax.ShapeDtypeStruct((n, columns, columns), F32),
         ),
         in_specs=[anywhere, anywhere, pl.BlockSpec(memory_space=pltpu.SMEM), anywhere, anywhere],
-        out_specs=(anywhere, anywhere),
+        out_specs=(pl.BlockSpec(memory_space=pltpu.VMEM),) * 2,
         scratch_shapes=scratch,
         compiler_params=pltpu.CompilerParams(
-            collective_id=0, has_side_effects=True, vmem_limit_bytes=60 * 1024 * 1024
+            collective_id=0, has_side_effects=True, vmem_limit_bytes=63 * 1024 * 1024
         ),
     )(subspace, inverse[0], weights, diag_tiles, upper_tiles)
 

time: 139 us -> 135 us (0.971)
  Pallas kernels: 134 us -> 131 us
    pallas_call x1, Pallas kernels: 134 us -> 131 us  [per_device(): pl.pallas_call(functools.partial(kernel, nodes, parts, 1.0 / (rows * part...]
where the time goes in v1:
time: 135 us
  Pallas kernels  131 us (97%)
  local copies, waits for them, and re-layouts  3.93 us (3%)
    pallas_call x1, Pallas kernels, per_device(): pl.pallas_call(functools.partial(kernel, nodes, parts, 1.0 / (rows * part...  131 us
    unnamed x2, local copies, waits for them, and re-layouts  3.93 us

profile of v1, /device:TPU:1, one launch (start us, length us, event | category | flops | bytes accessed | tf_op | source)
XLA Modules:
  0.0 135.3 jit_solution(2347956092050065015)
XLA Ops:
  0.6 130.7 %shard_map.68 = (f32[768,256]{1,0:T(8,128)}, f32[2,256,256]{2,1,0:T(8,128)}) custom-call(bf16[768,256]{1,0:T(8,128)(2,1)} %subspace.1, bf16[2,768,768]{2,1,0:T(8,128)(2,1)} %bitcast.1, f32[1,2]{1,0:T(1,128)} %weights.1, f32[768,128]{1,0:T(8,128)} %diag_in.1, f32[768,128]{1,0:T(8,128)} %upper_in.1), custom_call_target="tpu_custom_call" | custom-call | tf_op jit(solution)/shard_map/pallas_call | solution.py:524
  131.3 2.1 %copy.9 = f32[768,256]{1,0:T(8,128)} copy(f32[768,256]{1,0:T(8,128)} %get-tuple-element.4) | data formatting | bytes 1572864
  133.4 1.9 %copy.10 = f32[2,256,256]{2,1,0:T(8,128)} copy(f32[2,256,256]{2,1,0:T(8,128)} %get-tuple-element.5) | data formatting | bytes 1048576

commit v2 on v1

--- a/solution.py
+++ b/solution.py
@@ -446,6 +446,7 @@
             imaged[rows, :] = dot(0.5 * diag[rows, :], whole[rows, :], 1, 0, precise) + dot(
                 upper[rows, :], whole[t * band + band : t * band + 2 * band, :], 1, 0, precise
             )
+        all_finish(it, 0)
         rows = slice(size - band, size)
         near = dot(0.5 * diag[rows, :], whole[rows, :], 1, 0, precise)
         row_copy(it).wait_recv()
@@ -453,10 +454,6 @@
         imaged[rows, :] = near + dot(upper[rows, :], after, 1, 0, precise)
         product = dot(whole, imaged[...], 0, 0, precise)
         pack_start(it, 1, product + product.T)
-
-        all_finish(it, 0)
-        pack_sum(it, 1)
-        z_start(it, 1, pk[1, j, slice_rows, :])
         first, second, last = summed(it, 0)
         a[0, :half, :] = first * scale
         a[1, :half, :] = second * scale
@@ -464,7 +461,10 @@
         a[1, half:, :] = last * scale
         steps = columns // 8
         for k in range(steps):
-            if k == (3 * steps) // 4 - 1:
+            if k == steps // 8 - 1:
+                pack_sum(it, 1)
+                z_start(it, 1, pk[1, j, slice_rows, :])
+            if k == (13 * steps) // 16:
                 z_finish(it, 1)
             panel_step(a, k, columns)
         rows = lax.broadcasted_iota(jnp.int32, (columns, columns), 0)
@@ -489,6 +489,41 @@
     project(ITERS - 1)
     projected_drained(ITERS - 1)
     drained(ITERS - 1)
+
+
+def finish_kernel(ortho, projected, ortho_out, projected_out, ortho_held, projected_held, come, go):
+    count = come.shape[0] // 2
+    rows = ortho.shape[0] // count
+    wide = projected.shape[1] // count
+    places = []
+    for k in range(count):
+        at = pl.ds(k * rows, rows)
+        places.append((ortho.at[at], ortho_held.at[at], ortho_out.at[at]))
+    for k in range(count):
+        at = pl.ds(k * wide, wide)
+        places.append((projected.at[:, at], projected_held.at[:, at], projected_out.at[:, at]))
+    into = [pltpu.make_async_copy(a, b, come.at[k]) for k, (a, b, _) in enumerate(places)]
+    onward = [pltpu.make_async_copy(b, c, go.at[k]) for k, (_, b, c) in enumerate(places)]
+    for item in into:
+        item.start()
+    for first, second in zip(into, onward):
+        first.wait()
+        second.start()
+    for item in onward:
+        item.wait()
+
+
+def finished(ortho, projected):
+    anywhere = pl.BlockSpec(memory_space=pl.ANY)
+    return pl.pallas_call(
+        finish_kernel,
+        out_shape=tuple(jax.ShapeDtypeStruct(v.shape, v.dtype) for v in (ortho, projected)),
+        in_specs=[anywhere] * 2,
+        out_specs=(anywhere,) * 2,
+        scratch_shapes=[pltpu.VMEM(v.shape, v.dtype) for v in (ortho, projected)]
+        + [pltpu.SemaphoreType.DMA((8,))] * 2,
+        compiler_params=pltpu.CompilerParams(vmem_limit_bytes=62 * 1024 * 1024),
+    )(ortho, projected)
 
 
 def per_device(subspace, inverse, weights, diag_tiles, upper_tiles):
@@ -521,7 +556,7 @@
     scratch += [dma((n, side))] * 12
     scratch += [dma((n,)), dma((n,)), dma((n, 2)), dma((n, 2)), dma((n, nodes)), dma((n, nodes))]
     scratch += [dma((n, 2, chips))] * 2 + [dma((n, 2, nodes))] * 2 + [dma((n, 2))] * 2
-    return pl.pallas_call(
+    results = pl.pallas_call(
         functools.partial(kernel, nodes, parts, 1.0 / (rows * parts)),
         out_shape=(
             jax.ShapeDtypeStruct((rows, columns), F32),
@@ -531,9 +566,10 @@
         out_specs=(pl.BlockSpec(memory_space=pltpu.VMEM),) * 2,
         scratch_shapes=scratch,
         compiler_params=pltpu.CompilerParams(
-            collective_id=0, has_side_effects=True, vmem_limit_bytes=63 * 1024 * 1024
+            collective_id=0, has_side_effects=True, vmem_limit_bytes=62 * 1024 * 1024
         ),
     )(subspace, inverse[0], weights, diag_tiles, upper_tiles)
+    return finished(*results)
 
 
 def solution(mesh):

time: 135 us -> 133 us (0.985)
  local copies, waits for them, and re-layouts: 3.93 us -> 0 us
    unnamed x2 -> x0, local copies, waits for them, and re-layouts: 3.93 us -> none
    pallas_call x0 -> x1, Pallas kernels: none -> 2.21 us  [finished(): pl.pallas_call(finish_kernel, out_shape=tuple((jax.ShapeDtypeStruct(v.sha...]
where the time goes in v2:
time: 133 us
  Pallas kernels  132 us (99%)
    pallas_call x1, Pallas kernels, per_device(): pl.pallas_call(functools.partial(kernel, nodes, parts, 1.0 / (rows * part...  130 us

profile of v2, /device:TPU:1, one launch (start us, length us, event | category | flops | bytes accessed | tf_op | source)
XLA Modules:
  0.0 132.6 jit_solution(17236603922312602215)
XLA Ops:
  0.6 129.7 %shard_map.68 = (f32[768,256]{1,0:T(8,128)}, f32[2,256,256]{2,1,0:T(8,128)}) custom-call(bf16[768,256]{1,0:T(8,128)(2,1)} %subspace.1, bf16[2,768,768]{2,1,0:T(8,128)(2,1)} %bitcast.1, f32[1,2]{1,0:T(1,128)} %weights.1, f32[768,128]{1,0:T(8,128)} %diag_in.1, f32[768,128]{1,0:T(8,128)} %upper_in.1), custom_call_target="tpu_custom_call" | custom-call | tf_op jit(solution)/shard_map/pallas_call | solution.py:559
  130.4 2.2 %shard_map.69 = (f32[768,256]{1,0:T(8,128)}, f32[2,256,256]{2,1,0:T(8,128)}) custom-call(f32[768,256]{1,0:T(8,128)} %get-tuple-element.4.ortho, f32[2,256,256]{2,1,0:T(8,128)} %get-tuple-element.5.projected), custom_call_target="tpu_custom_call" | custom-call | tf_op jit(solution)/shard_map/pallas_call | solution.py:518

commit v3 on v2

--- a/solution.py
+++ b/solution.py
@@ -31,7 +31,7 @@
     r0 = 8 * k
     half, lane0 = r0 // 128, r0 % 128
     halves = size // 128
-    row = [[jnp.broadcast_to(a[h, r0 + i : r0 + i + 1, :], (8, 128)) for h in range(halves)] for i in range(8)]
+    row = [[a[h, pl.ds(r0 + i, 8, stride=0), :] for h in range(halves)] for i in range(8)]
     e = [
         [jnp.broadcast_to(row[i][half][:, lane0 + j : lane0 + j + 1], (8, 128)) for j in range(i + 1)]
         for i in range(8)

time: 133 us -> 132 us (level)
  no operation moved by 1% of the time
where the time goes in v3:
time: 132 us; the launch traced here: 131 us
  Pallas kernels  131 us (99%)
    pallas_call x1, Pallas kernels, per_device(): pl.pallas_call(functools.partial(kernel, nodes, parts, 1.0 / (rows * part...  129 us

profile of v3, /device:TPU:1, one launch (start us, length us, event | category | flops | bytes accessed | tf_op | source)
XLA Modules:
  0.0 131.4 jit_solution(4539141903421659325)
XLA Ops:
  0.6 128.5 %shard_map.68 = (f32[768,256]{1,0:T(8,128)}, f32[2,256,256]{2,1,0:T(8,128)}) custom-call(bf16[768,256]{1,0:T(8,128)(2,1)} %subspace.1, bf16[2,768,768]{2,1,0:T(8,128)(2,1)} %bitcast.1, f32[1,2]{1,0:T(1,128)} %weights.1, f32[768,128]{1,0:T(8,128)} %diag_in.1, f32[768,128]{1,0:T(8,128)} %upper_in.1), custom_call_target="tpu_custom_call" | custom-call | tf_op jit(solution)/shard_map/pallas_call | solution.py:559
  129.1 2.2 %shard_map.69 = (f32[768,256]{1,0:T(8,128)}, f32[2,256,256]{2,1,0:T(8,128)}) custom-call(f32[768,256]{1,0:T(8,128)} %get-tuple-element.4.ortho, f32[2,256,256]{2,1,0:T(8,128)} %get-tuple-element.5.projected), custom_call_target="tpu_custom_call" | custom-call | tf_op jit(solution)/shard_map/pallas_call | solution.py:518
